TPU v7x, 32 devices: a whole 2x2x4 slice. The times are simulated.
32 devices in a mesh: phase: 2 (over x), ctx: 8 (over z, core), mp: 2 (over y).
Axes of the slice: x: 2, y: 2, z: 4, core: 2. Of those that a mesh axis runs over, the one named last changes fastest.
Arguments:
- streams: bfloat16 [2, 1536, 3, 8192], P('phase', 'ctx', None, 'mp'), may hold values from -12 to 12
- doc_ids: int32 [1536], replicated, may hold values from 0 to 3, never falling along the last dimension, each value on 1 to 768 neighbouring positions
- feat_short: float32 [3, 3, 8192], P(None, None, 'mp'), may hold values from -3 to 3
- filt_short: float32 [7, 8192], P(None, 'mp'), may hold values from -2 to 2
- feat_medium: float32 [3, 3, 8192], P(None, None, 'mp'), may hold values from -3 to 3
- filt_medium: float32 [128, 8192], P(None, 'mp'), may hold values from -0.75 to 0.75
- medium_rates: float32 [8192], P('mp'), may hold values from 0.004 to 0.12
Outputs:
- next_state: bfloat16 [2, 1536, 3, 8192], P('phase', 'ctx', None, 'mp')
Inputs may be any that keep to these rules, and one draw needn't show every extreme that they name: `doc_ids`: document ids never fall along the context, and no document is longer than half of 1536 positions.
All inputs are finite; a program needn't handle non-finite values.
Results may differ from a plain program's by a relative error of at most 0.008.
Values may be sent and summed in bfloat16 or wider, within the bound.
A program may use at most 192 MiB of HBM per device.

v0:
```python
import math

import jax
import jax.numpy as jnp
from jax import lax
from jax.sharding import PartitionSpec as P

HEAD_DIM = 128
QBLOCK = 768


def shifted(array, axis, by):
    peers = lax.axis_size(axis)
    pairs = [(i, i + by) for i in range(peers) if 0 <= i + by < peers]
    return lax.ppermute(array, axis, pairs)


def swapped(array, axis, bit):
    return lax.ppermute(array, axis, [(i, i ^ 1 << bit) for i in range(lax.axis_size(axis))])


def featurize(extended, taps_weight):
    widened = extended.astype(jnp.float32)
    return (
        taps_weight[:, 0] * widened[2:]
        + taps_weight[:, 1] * widened[1:-1]
        + taps_weight[:, 2] * widened[:-2]
    )


def causal_rows(product, filter_taps):
    kernel = filter_taps[::-1][:, None, :]
    conv_result = lax.conv_general_dilated(
        product.astype(jnp.float32)[None],
        kernel,
        (1,),
        "VALID",
        dimension_numbers=("NWC", "WIO", "NWC"),
        feature_group_count=filter_taps.shape[1],
        precision=lax.Precision.HIGHEST,
    )
    return conv_result[0]


def conv_block(extended, taps_weight, filter_taps):
    row_total = extended.shape[0] - 1 - filter_taps.shape[0]
    features = featurize(extended, taps_weight)
    product = (features[:, 1] * features[:, 2]).astype(jnp.bfloat16)
    mixed_rows = causal_rows(product, filter_taps)
    query_feat = features[-row_total:, 0]
    value_sum = extended[-row_total:, 2].astype(jnp.float32) + query_feat * mixed_rows
    return jnp.stack([query_feat, features[-row_total:, 1], value_sum], 1).astype(jnp.bfloat16)


def attend(packed, doc_ids, row_total):
    key_rows = packed[:, 1]
    value_rows = packed[:, 2]
    seq_total = packed.shape[0]
    head_count = packed.shape[2]
    head_depth = packed.shape[3]
    query_rows = packed[:, 0]
    query_blocks = query_rows.reshape(row_total // QBLOCK, QBLOCK, head_count, head_depth)
    key_pos = jnp.arange(seq_total, dtype=jnp.int32)
    score_scale = 1.0 / math.sqrt(head_depth)

    def score_block(block_pair):
        query_block, first_row = block_pair
        scores = (
            jnp.einsum("qhd,khd->hqk", query_block, key_rows, preferred_element_type=jnp.float32)
            * score_scale
        )
        query_pos = first_row + jnp.arange(QBLOCK, dtype=jnp.int32)
        query_doc = lax.dynamic_slice_in_dim(doc_ids, first_row, QBLOCK, 0)
        allowed = (key_pos[None, :] <= query_pos[:, None]) & (
            doc_ids[None, :] == query_doc[:, None]
        )
        scores = jnp.where(allowed[None], scores, -1e30)
        row_max = jnp.max(scores, axis=2, keepdims=True)
        exponent = jnp.exp(scores - row_max)
        weights = (exponent / jnp.sum(exponent, axis=2, keepdims=True)).astype(jnp.bfloat16)
        return jnp.einsum(
            "hqk,khd->qhd", weights, value_rows, preferred_element_type=jnp.float32
        ).astype(jnp.bfloat16)

    first_rows = QBLOCK * jnp.arange(row_total // QBLOCK, dtype=jnp.int32)
    attended = lax.map(score_block, (query_blocks, first_rows))
    return attended.reshape(row_total, head_count, head_depth)


def local(streams, doc_ids, feat_short, filt_short, feat_medium, filt_medium, medium_rates):
    local_state = streams[0]
    row_count = local_state.shape[0]
    channels = local_state.shape[2]
    phase_index = lax.axis_index("phase")
    short_len = filt_short.shape[0]
    medium_len = filt_medium.shape[0]
    taps = jnp.arange(medium_len, dtype=jnp.float32)
    medium_filter = filt_medium * jnp.exp(-medium_rates[None, :] * taps[:, None])
    halo_rows = shifted(local_state[row_count - short_len - 1 :], "ctx", 1)
    short_out = conv_block(jnp.concatenate([halo_rows, local_state], 0), feat_short, filt_short)
    earlier_rows = shifted(short_out[row_count - medium_len - 1 :], "ctx", 1)
    conv_out = conv_block(jnp.concatenate([earlier_rows, short_out], 0), feat_medium, medium_filter)
    ctx_count = lax.axis_size("ctx")
    group_heads = channels // (HEAD_DIM * ctx_count)
    seq_total = row_count * ctx_count
    packed = local_state.reshape(row_count, 3, ctx_count, group_heads, HEAD_DIM)
    head_streams = lax.all_to_all(packed, "ctx", split_axis=2, concat_axis=0, tiled=True)[:, :, 0]
    item_count = head_streams.shape[2]

    def compute_rows(operand):
        return attend(operand, doc_ids, seq_total)

    def skip_rows(operand):
        return jnp.zeros((seq_total, item_count, HEAD_DIM), jnp.bfloat16)

    attended = lax.cond(phase_index == 1, compute_rows, skip_rows, head_streams)
    attended_back = lax.all_to_all(attended, "ctx", split_axis=0, concat_axis=1, tiled=True)
    attention_rows = attended_back.reshape(row_count, channels)
    value_sum = (local_state[:, 2].astype(jnp.float32) + attention_rows.astype(jnp.float32)).astype(
        jnp.bfloat16
    )
    attn_state = jnp.stack([local_state[:, 0], local_state[:, 1], value_sum], 1)
    outgoing = jnp.where(phase_index == 0, conv_out, attn_state)
    incoming = swapped(outgoing, "phase", 0)
    return incoming[None]


def solution(mesh):
    in_specs = (
        P("phase", "ctx", None, "mp"),
        P(),
        P(None, None, "mp"),
        P(None, "mp"),
        P(None, None, "mp"),
        P(None, "mp"),
        P("mp"),
    )
    out_specs = P("phase", "ctx", None, "mp")
    return jax.shard_map(local, mesh=mesh, in_specs=in_specs, out_specs=out_specs, check_vma=False)
```

profile of v0, /device:TPU:10, one launch (start us, length us, event | category | flops | bytes accessed | tf_op | source)
XLA Modules:
  0.0 589.5 jit_solution(5228509431510301562)
XLA Ops:
  0.0 8.7 %reshape_squeeze.3 = bf16[192,3,8,4,128]{4,3,2,0,1:T(4,128)(2,1)} reshape(bf16[1,192,3,4096]{3,1,2,0:T(8,128)(2,1)} %param.11) | data formatting | bytes 9437184 | tf_op jit(solution)/shard_map/reshape;squeeze | solution.py:106
  8.7 6.9 %copy.42 = bf16[192,3,8,4,128]{4,3,0,1,2:T(4,128)(2,1)} copy(bf16[192,3,8,4,128]{4,3,2,0,1:T(4,128)(2,1)} %reshape_squeeze.3) | data formatting | bytes 9437184 | tf_op jit(solution)/shard_map/reshape;squeeze | solution.py:106
  15.6 5.3 all-to-all-start
  20.9 6.4 %copy.76 = bf16[1,192,3,4096]{3,2,1,0:T(4,128)(2,1)S(1)} copy(bf16[1,192,3,4096]{3,1,2,0:T(8,128)(2,1)} %param.11) | data formatting | bytes 9437184 | tf_op args[0]
  27.4 2.7 copy-done
  30.2 2.0 collective-permute-start
  33.1 9.5 %rev.6 = f32[7,4096]{1,0:T(8,128)} reverse(f32[7,4096]{1,0:T(8,128)S(1)} %copy-done.11), dimensions={0} | reverse | bytes 229376 | tf_op jit(solution)/shard_map/rev | solution.py:32
  43.3 57.9 %collective-permute-done = bf16[8,3,4096]{2,1,0:T(4,128)(2,1)S(1)} collective-permute-done((bf16[8,3,4096]{2,1,0:T(4,128)(2,1)S(1)}, bf16[8,3,4096]{2,1,0:T(4,128)(2,1)S(1)}, u32[]{:S(2)}, u32[]{:S(2)}) %collective-permute-start) | collective-permute-done | bytes 196640 | tf_op jit(solution)/shard_map/ppermute | solution.py:15
  101.2 10.1 %maximum_convert_fusion.1 = f32[200,3,4096]{2,1,0:T(4,128)} fusion(bf16[192,3,4096]{2,1,0:T(4,128)(2,1)} %bitcast.101, bf16[8,3,4096]{2,1,0:T(4,128)(2,1)S(1)} %collective-permute-done), kind=kLoop, calls=%fused_computation.40 | loop fusion | flops 4915200 | bytes 14745600 | tf_op jit(solution)/shard_map/convert_element_type | solution.py:23
  111.3 11.5 %all-to-all-done = bf16[192,3,8,4,128]{4,3,0,1,2:T(4,128)(2,1)} async-done(((bf16[192,3,8,4,128]{4,3,0,1,2:T(4,128)(2,1)}), bf16[192,3,8,4,128]{4,3,0,1,2:T(4,128)(2,1)}, u32[]{:S(2)}, u32[]{:S(2)}) %all-to-all-start) | async-done | bytes 4718624 | tf_op jit(solution)/shard_map/all_to_all | solution.py:107
  122.8 60.5 %conditional.1 = (bf16[1536,4,128]{2,1,0:T(4,128)(2,1)}) conditional(s32[]{:T(128)} %convert_element_type.89, () %tuple.15, (bf16[8,192,3,1,4,128]{5,4,1,2,0,3:T(4,128)(2,1)}, s32[1536]{0:T(1024)}) %tuple.16), branch_computations={%region_0.0_spmd, %region_1.6_spmd} | conditional | flops 2448165120 | bytes 65344816 | solution.py:116
  122.9 3.5 copy.43
  126.5 2.0 slice_bitcast_fusion
  128.5 54.8 %while.10 = (s32[]{:T(128)}, bf16[2,768,4,128]{3,2,1,0:T(4,128)(2,1)}, s32[2]{0:T(128)S(1)}, s32[1536]{0:T(1024)S(1)}, bf16[2,768,4,128]{3,1,0,2:T(8,128)(2,1)},...) while((s32[]{:T(128)}, ...), condition=%wide.region_5.5_spmd.clone, body=%wide.region_2.4_spmd.clone.sunk | while | flops 2448165120 | bytes 46445740 | solution.py:86
  132.0 1.3 fusion.88
  133.4 12.0 %fusion.89 = (f32[4,768]{1,0:T(4,128)S(1)}, f32[4,768,1536]{2,1,0:T(8,128)}) fusion(pred[768,1536]{1,0:T(8,128)(4,1)S(1)} %fusion.88, bf16[1536,4,128]{2,0,1:T(8,128)(2,1)} %get-tuple-element.198, bf16[2,768,4,128]{3,1,0,2:T(8,128)(2,1)} %get-tuple-element.197, s32[]{:T(128)S(6)} %copy.82), kind=kOutput, calls=%fused_computation.86.clone.1 | convolution fusion | flops 1226835456 | bytes 22425604 | tf_op jit(solution)/shard_map/cond/branch_1_fun/while/body/eval_jaxpr/sub | solution.py:79
  145.3 9.0 %fusion.90 = bf16[1,768,4,128]{3,1,2,0:T(8,128)(2,1)S(1)} fusion(bf16[1536,4,128]{2,0,1:T(8,128)(2,1)S(1)} %get-tuple-element.199, f32[4,768,1536]{2,1,0:T(8,128)} %get-tuple-element.171, f32[4,768]{1,0:T(4,128)S(1)} %get-tuple-element.172), kind=kOutput, calls=%fused_computation.14.clone.1 | convolution fusion | flops 1217789952 | bytes 21245952 | tf_op jit(solution)/shard_map/cond/branch_1_fun/while/body/eval_jaxpr/hqk,khd->qhd/dot_general | solution.py:81
  154.4 1.5 copy_dynamic-update-slice_fusion.2
  159.4 1.3 fusion.88
  160.7 12.0 %fusion.89 = (f32[4,768]{1,0:T(4,128)S(1)}, f32[4,768,1536]{2,1,0:T(8,128)}) fusion(pred[768,1536]{1,0:T(8,128)(4,1)S(1)} %fusion.88, bf16[1536,4,128]{2,0,1:T(8,128)(2,1)} %get-tuple-element.198, bf16[2,768,4,128]{3,1,0,2:T(8,128)(2,1)} %get-tuple-element.197, s32[]{:T(128)S(6)} %copy.82), kind=kOutput, calls=%fused_computation.86.clone.1 | convolution fusion | flops 1226835456 | bytes 22425604 | tf_op jit(solution)/shard_map/cond/branch_1_fun/while/body/eval_jaxpr/sub | solution.py:79
  172.7 9.0 %fusion.90 = bf16[1,768,4,128]{3,1,2,0:T(8,128)(2,1)S(1)} fusion(bf16[1536,4,128]{2,0,1:T(8,128)(2,1)S(1)} %get-tuple-element.199, f32[4,768,1536]{2,1,0:T(8,128)} %get-tuple-element.171, f32[4,768]{1,0:T(4,128)S(1)} %get-tuple-element.172), kind=kOutput, calls=%fused_computation.14.clone.1 | convolution fusion | flops 1217789952 | bytes 21245952 | tf_op jit(solution)/shard_map/cond/branch_1_fun/while/body/eval_jaxpr/hqk,khd->qhd/dot_general | solution.py:81
  181.8 1.5 copy_dynamic-update-slice_fusion.2
  183.3 18.0 %all-to-all-start.1 = ((bf16[1536,4,128]{2,1,0:T(4,128)(2,1)}), bf16[1536,4,128]{2,1,0:T(4,128)(2,1)}, u32[]{:S(2)}, u32[]{:S(2)}) async-start(bf16[1536,4,128]{2,1,0:T(4,128)(2,1)} %get-tuple-element.203), calls=%async_computation.1 | async-start | bytes 3145728 | tf_op jit(solution)/shard_map/all_to_all | solution.py:117
  201.3 21.1 %fusion.32 = f32[198,3,4096]{2,1,0:T(4,128)} fusion(f32[200,3,4096]{2,1,0:T(4,128)} %maximum_convert_fusion.1, f32[3,4096]{1,0:T(4,128)S(1)} %copy-done.8, f32[3,4096]{1,0:T(4,128)S(1)} %copy-done.9, f32[3,4096]{1,0:T(4,128)S(1)} %bitcast.112), kind=kLoop, calls=%fused_computation.35 | loop fusion | flops 12165120 | bytes 39075840 | tf_op jit(solution)/shard_map/add | solution.py:25
  222.4 7.7 %slice.215 = bf16[192,2,4096]{2,1,0:T(2,128)(2,1)S(1)} slice(f32[198,3,4096]{2,1,0:T(4,128)} %fusion.32), slice={[6:198], [0:2], [0:4096]} | slice | bytes 6291456 | tf_op jit(solution)/shard_map/slice | solution.py:50
  230.2 13.9 %fusion.43 = bf16[198,1,4096]{2,1,0:T(2,128)(2,1)S(1)} fusion(f32[198,3,4096]{2,1,0:T(4,128)} %fusion.32), kind=kLoop, calls=%fused_computation.55 | loop fusion | flops 1622016 | bytes 8110080 | tf_op jit(solution)/shard_map/convert_element_type | solution.py:48
  244.0 1.8 copy.73
  245.8 1.3 pad
  247.1 3.3 reshape.139
  250.4 2.5 copy.36
  253.1 1.7 convolution_select_fusion
  254.8 4.0 copy.38
  258.7 6.5 %reshape.149 = f32[1,200,4096]{2,0,1:T(1,128)} reshape(f32[8,25,4096]{2,1,0:T(8,128)} %copy.38) | data formatting | bytes 6553600 | tf_op jit(solution)/shard_map/conv_general_dilated | solution.py:33
  265.2 2.4 copy.44
  267.6 13.5 %add_convert_fusion = (bf16[192,1,4096]{2,1,0:T(2,128)(2,1)}, bf16[192,1,4096]{2,1,0:T(2,128)(2,1)S(1)}) fusion(f32[192,1,4096]{2,1,0:T(1,128)S(1)} %bitcast.107, bf16[192,3,4096]{2,1,0:T(4,128)(2,1)} %bitcast.102, f32[1,200,4096]{2,0,1:T(1,128)S(1)} %copy-done.3, f32[198,3,4096]{2,1,0:T(4,128)} %fusion.32), kind=kLoop, calls=%fused_computation.62 | loop fusion | flops 4718592 | bytes 14155776 | tf_op jit(solution)/shard_map/convert_element_type | solution.py:119
  281.1 6.5 %pad_maximum_fusion = bf16[129,3,4096]{2,1,0:T(4,128)(2,1)} fusion(bf16[192,1,4096]{2,1,0:T(2,128)(2,1)S(1)} %get-tuple-element.113, bf16[192,2,4096]{2,1,0:T(2,128)(2,1)S(1)} %slice.215), kind=kLoop, calls=%fused_computation.51 | loop fusion | flops 6340608 | bytes 7888896 | tf_op jit(solution)/shard_map/stack | solution.py:52
  287.7 2.1 collective-permute-start.1
  289.9 4.8 slice.143
  296.0 3.3 exponential_multiply_fusion
  299.3 16.9 %rev.7 = f32[128,4096]{1,0:T(8,128)} reverse(f32[128,4096]{1,0:T(8,128)} %exponential_multiply_fusion), dimensions={0} | reverse | bytes 4194304 | tf_op jit(solution)/shard_map/rev | solution.py:32
  316.2 22.1 %collective-permute-done.1 = bf16[129,3,4096]{2,1,0:T(4,128)(2,1)} collective-permute-done((bf16[129,3,4096]{2,1,0:T(4,128)(2,1)}, bf16[129,3,4096]{2,1,0:T(4,128)(2,1)}, u32[]{:S(2)}, u32[]{:S(2)}) %collective-permute-start.1) | collective-permute-done | bytes 3170336 | tf_op jit(solution)/shard_map/ppermute | solution.py:15
  338.3 14.2 %maximum_convert_fusion = f32[321,3,4096]{2,1,0:T(4,128)} fusion(bf16[192,1,4096]{2,1,0:T(2,128)(2,1)} %copy-done.1, bf16[192,2,4096]{2,1,0:T(2,128)(2,1)S(1)} %slice.215, bf16[129,3,4096]{2,1,0:T(4,128)(2,1)} %collective-permute-done.1), kind=kLoop, calls=%fused_computation.39 | loop fusion | flops 23666688 | bytes 23666688 | tf_op jit(solution)/shard_map/convert_element_type | solution.py:23
  352.5 28.5 %fusion.30 = f32[319,3,4096]{2,1,0:T(4,128)} fusion(f32[321,3,4096]{2,1,0:T(4,128)} %maximum_convert_fusion, f32[3,4096]{1,0:T(4,128)S(1)} %get-tuple-element.124, f32[3,4096]{1,0:T(4,128)S(1)} %get-tuple-element.125, f32[3,4096]{1,0:T(4,128)S(1)} %bitcast.113), kind=kLoop, calls=%fused_computation.30 | loop fusion | flops 19599360 | bytes 62865408 | tf_op jit(solution)/shard_map/add | solution.py:25
  381.0 9.5 %slice.214 = bf16[192,2,4096]{2,1,0:T(2,128)(2,1)} slice(f32[319,3,4096]{2,1,0:T(4,128)} %fusion.30), slice={[127:319], [0:2], [0:4096]} | slice | bytes 6291456 | tf_op jit(solution)/shard_map/slice | solution.py:50
  390.5 43.1 %fusion.47 = bf16[192,1,4096]{2,1,0:T(2,128)(2,1)S(1)} fusion(f32[319,3,4096]{2,1,0:T(4,128)} %fusion.30, bf16[192,1,4096]{2,1,0:T(2,128)(2,1)S(1)} %copy-done.2, f32[128,1,4096]{2,0,1:T(8,128)} %bitcast.110), kind=kOutput, calls=%fused_computation.63 | convolution fusion | flops 1213718528 | bytes 18841600 | tf_op jit(solution)/shard_map/conv_general_dilated | solution.py:33
  433.7 13.3 %maximum_select_fusion = bf16[192,3,4096]{2,1,0:T(4,128)(2,1)S(1)} fusion(bf16[192,1,4096]{2,1,0:T(2,128)(2,1)S(1)} %fusion.47, bf16[192,2,4096]{2,1,0:T(2,128)(2,1)S(1)} %copy-done.6, bf16[192,1,4096]{2,1,0:T(2,128)(2,1)S(1)} %copy-done.4, bf16[192,2,4096]{2,1,0:T(2,128)(2,1)S(1)} %copy-done.5, pred[]{:T(512)S(6)} %eq.23), kind=kLoop, calls=%fused_computation.43 | loop fusion | flops 21233664 | bytes 14155777 | tf_op jit(solution)/shard_map/jit(_where)/select_n | solution.py:123
  447.1 136.6 %collective-permute-done.2 = bf16[192,3,4096]{2,1,0:T(4,128)(2,1)S(1)} collective-permute-done((bf16[192,3,4096]{2,1,0:T(4,128)(2,1)S(1)}, bf16[192,3,4096]{2,1,0:T(4,128)(2,1)S(1)}, u32[]{:S(2)}, u32[]{:S(2)}) %collective-permute-start.2) | collective-permute-done | bytes 4718624 | tf_op jit(solution)/shard_map/ppermute | solution.py:19
  583.7 5.6 copy.45
  (55 shorter events, 6.1 us)
Async XLA Ops:
  15.6 107.1 %all-to-all-start = ((bf16[192,3,8,4,128]{4,3,0,1,2:T(4,128)(2,1)}), bf16[192,3,8,4,128]{4,3,0,1,2:T(4,128)(2,1)}, u32[]{:S(2)}, u32[]{:S(2)}) async-start(bf16[192,3,8,4,128]{4,3,0,1,2:T(4,128)(2,1)} %copy.42), calls=%async_computation | async-start | bytes 9437184 | tf_op jit(solution)/shard_map/all_to_all | solution.py:107
  20.9 11.3 %copy-start.13 = (f32[3,3,4096]{2,1,0:T(4,128)S(1)}, f32[3,3,4096]{2,1,0:T(4,128)}, u32[]{:S(2)}) copy-start(f32[3,3,4096]{2,1,0:T(4,128)} %param.13) | copy-start | bytes 442372
  20.9 12.2 %copy-start.11 = (f32[7,4096]{1,0:T(8,128)S(1)}, f32[7,4096]{1,0:T(8,128)}, u32[]{:S(2)}) copy-start(f32[7,4096]{1,0:T(8,128)} %param.14) | copy-start | bytes 344068
  27.4 2.7 copy-start
  30.2 71.0 %collective-permute-start = (bf16[8,3,4096]{2,1,0:T(4,128)(2,1)S(1)}, bf16[8,3,4096]{2,1,0:T(4,128)(2,1)S(1)}, u32[]{:S(2)}, u32[]{:S(2)}) collective-permute-start(bf16[8,3,4096]{2,1,0:T(4,128)(2,1)S(1)} %slice_bitcast_fusion.3), channel_id=1, source_target_pairs={{0,2},{2,4},{4,6},{6,8},{8,10},{10,12},{12,14},{1,3},{3,5},{5,7},{... | collective-permute-start | bytes 589832 | tf_op jit(solution)/shard_map/ppermute | solution.py:15
  122.8 78.5 %copy-start.8 = (f32[3,4096]{1,0:T(4,128)S(1)}, f32[3,4096]{1,0:T(4,128)}, u32[]{:S(2)}) copy-start(f32[3,4096]{1,0:T(4,128)} %get-tuple-element.122) | copy-start | bytes 147460
  122.8 78.5 %copy-start.9 = (f32[3,4096]{1,0:T(4,128)S(1)}, f32[3,4096]{1,0:T(4,128)}, u32[]{:S(2)}) copy-start(f32[3,4096]{1,0:T(4,128)} %get-tuple-element.123) | copy-start | bytes 147460
  122.8 78.5 %copy-start.10 = (f32[3,1,4096]{2,0,1:T(4,128)S(1)}, f32[3,1,4096]{2,0,1:T(4,128)}, u32[]{:S(2)}) copy-start(f32[3,1,4096]{2,0,1:T(4,128)} %copy.74) | copy-start | bytes 147460
  126.5 2.0 copy-start.7
  183.3 82.0 %all-to-all-start.1 = ((bf16[1536,4,128]{2,1,0:T(4,128)(2,1)}), bf16[1536,4,128]{2,1,0:T(4,128)(2,1)}, u32[]{:S(2)}, u32[]{:S(2)}) async-start(bf16[1536,4,128]{2,1,0:T(4,128)(2,1)} %get-tuple-element.203), calls=%async_computation.1 | async-start | bytes 3145728 | tf_op jit(solution)/shard_map/all_to_all | solution.py:117
  247.1 6.0 %copy-start.12 = (f32[7,4096]{1,0:T(8,128)S(1)}, f32[7,4096]{1,0:T(8,128)}, u32[]{:S(2)}) copy-start(f32[7,4096]{1,0:T(8,128)} %rev.6) | copy-start | bytes 344068
  247.1 6.0 %copy-start.15 = (pred[8,25]{0,1:T(8,128)(4,1)S(1)}, pred[8,25]{0,1:T(8,128)(4,1)}, u32[]{:S(2)}) copy-start(pred[8,25]{0,1:T(8,128)(4,1)} %constant.47) | copy-start | bytes 604
  265.2 2.4 copy-start.3
  265.2 24.6 %slice-start = ((s8[6291456]{0:T(1024)(128)(4,1)}), s8[4194304]{0:T(1024)(128)(4,1)S(1)}, s32[]{:S(2)}) async-start(s8[6291456]{0:T(1024)(128)(4,1)} %bitcast.103), calls=%async_computation.2 | async-start | bytes 8388608
  267.6 22.2 %slice-start.1 = ((s8[6291456]{0:T(1024)(128)(4,1)}), s8[2097152]{0:T(1024)(128)(4,1)S(1)}, s32[]{:S(2)}) async-start(s8[6291456]{0:T(1024)(128)(4,1)} %bitcast.103), calls=%async_computation.3 | async-start | bytes 4194304
  281.1 6.6 %copy-start.1 = (bf16[192,1,4096]{2,1,0:T(2,128)(2,1)}, bf16[192,1,4096]{2,1,0:T(2,128)(2,1)S(1)}, u32[]{:S(2)}) copy-start(bf16[192,1,4096]{2,1,0:T(2,128)(2,1)S(1)} %get-tuple-element.113) | copy-start | bytes 4718596
  287.7 7.0 %copy-start.14 = (f32[4096]{0:T(1024)S(1)}, f32[4096]{0:T(1024)}, u32[]{:S(2)}) copy-start(f32[4096]{0:T(1024)} %param.17) | copy-start | bytes 49156
  287.7 50.6 %collective-permute-start.1 = (bf16[129,3,4096]{2,1,0:T(4,128)(2,1)}, bf16[129,3,4096]{2,1,0:T(4,128)(2,1)}, u32[]{:S(2)}, u32[]{:S(2)}) collective-permute-start(bf16[129,3,4096]{2,1,0:T(4,128)(2,1)} %pad_maximum_fusion), channel_id=1, source_target_pairs={{0,2},{2,4},{4,6},{6,8},{8,10},{10,12},{12,14},{1,3},{3,5},{5,7},{... | collective-permute-start | bytes 9510920 | tf_op jit(solution)/shard_map/ppermute | solution.py:15
  381.0 9.5 %copy-start.2 = (bf16[192,1,4096]{2,1,0:T(2,128)(2,1)S(1)}, bf16[192,1,4096]{2,1,0:T(2,128)(2,1)}, u32[]{:S(2)}) copy-start(bf16[192,1,4096]{2,1,0:T(2,128)(2,1)} %copy-done.1) | copy-start | bytes 4718596
  390.5 43.2 %copy-start.4 = (bf16[192,1,4096]{2,1,0:T(2,128)(2,1)S(1)}, bf16[192,1,4096]{2,1,0:T(2,128)(2,1)}, u32[]{:S(2)}) copy-start(bf16[192,1,4096]{2,1,0:T(2,128)(2,1)} %get-tuple-element.112) | copy-start | bytes 4718596
  390.5 43.2 %copy-start.5 = (bf16[192,2,4096]{2,1,0:T(2,128)(2,1)S(1)}, bf16[192,2,4096]{2,1,0:T(2,128)(2,1)}, u32[]{:S(2)}) copy-start(bf16[192,2,4096]{2,1,0:T(2,128)(2,1)} %slice.143) | copy-start | bytes 9437188
  390.5 43.2 %copy-start.6 = (bf16[192,2,4096]{2,1,0:T(2,128)(2,1)S(1)}, bf16[192,2,4096]{2,1,0:T(2,128)(2,1)}, u32[]{:S(2)}) copy-start(bf16[192,2,4096]{2,1,0:T(2,128)(2,1)} %slice.214) | copy-start | bytes 9437188
  447.0 136.6 %collective-permute-start.2 = (bf16[192,3,4096]{2,1,0:T(4,128)(2,1)S(1)}, bf16[192,3,4096]{2,1,0:T(4,128)(2,1)S(1)}, u32[]{:S(2)}, u32[]{:S(2)}) collective-permute-start(bf16[192,3,4096]{2,1,0:T(4,128)(2,1)S(1)} %maximum_select_fusion), channel_id=1, source_target_pairs={{0,16},{16,0},{1,17},{17,1},{2,18},{18,2},{3,19},{19,3},{4,20},{20... | collective-permute-start | bytes 14155784 | tf_op jit(solution)/shard_map/ppermute | solution.py:19
where the time goes:
time: 598 us; the launch traced here: 589 us
  waiting for transfers between devices  228 us (38%)
  other arithmetic  128 us (21%)
  local copies, waits for them, and re-layouts  114 us (19%)
  matrix products  86.9 us (15%)
  starting transfers between devices  27.6 us (5%)
    ppermute x1, waiting for transfers between devices, swapped(): lax.ppermute(array, axis, [(i, i ^ 1 << bit) for i in range(lax.axis_size...  137 us
    ppermute x2, waiting for transfers between devices, shifted(): return lax.ppermute(array, axis, pairs)  80 us
    add x2, other arithmetic, featurize(): taps_weight[:, 0] * widened[2:] + taps_weight[:, 1] * widened[1:-1]  49.7 us
    conv_general_dilated x2, matrix products, causal_rows(): lax.conv_general_dilated(product.astype(jnp.float32)[None], kernel, (1,),...  44.9 us
    rev x2, local copies, waits for them, and re-layouts, causal_rows(): kernel = filter_taps[::-1][:, None, :]  26.4 us
    convert_element_type x2, other arithmetic, featurize(): widened = extended.astype(jnp.float32)  24.3 us
    sub x2, matrix products, score_block(): exponent = jnp.exp(scores - row_max)  24 us
    dot_general x2, matrix products, score_block(): jnp.einsum('hqk,khd->qhd', weights, value_rows, preferred_element_type=jn...  18.1 us
  transfers between devices with their start and end apart: 5, of which 4 were waited for; matrix products, arithmetic and copies ran while one was open for 20% of the time, Pallas kernels for 0%

commit v1 on v0

v1 whole, which is shorter than its diff:
```python
import functools
import math

import jax
import jax.numpy as jnp
from jax import lax
from jax.experimental import pallas as pl
from jax.experimental.pallas import tpu as pltpu
from jax.sharding import PartitionSpec as P

HEAD_DIM = 128
CHUNKS = 4
HALO = 16
LANES = 128
MESH = pl.DeviceIdType.MESH


def feature(rows, weight, stream, count):
    first = rows.shape[0] - count
    return (
        weight[stream, 0][None] * rows[first:]
        + weight[stream, 1][None] * rows[first - 1 : first - 1 + count]
        + weight[stream, 2][None] * rows[first - 2 : first - 2 + count]
    )


def tick_kernel(
    hops,
    own_ref,
    other_ref,
    query_doc_ref,
    key_doc_ref,
    feat_ref,
    filt_ref,
    feat2_ref,
    filt2_ref,
    rate_ref,
    kept_ref,
    got_ref,
    state,
    chain,
    halo,
    halo2,
    past,
    short,
    tail,
    shift_ref,
    h_ref,
    bias_ref,
    local_sems,
    send_sems,
    recv_sems,
):
    rows = state.shape[2]
    half = state.shape[3]
    width = half // CHUNKS
    tiles = width // LANES
    taps = filt2_ref.shape[0]
    keys = rows * (hops + 1)
    phase = lax.axis_index("phase")
    place = lax.axis_index("ctx")
    peers = lax.axis_size("ctx")
    right = lax.rem(place + 1, peers)
    left = lax.rem(place + peers - 1, peers)
    partner = 1 - phase
    begin = place == 0

    load_own = pltpu.make_async_copy(own_ref, state.at[phase], local_sems.at[0])
    load_own.start()

    barrier = pltpu.get_barrier_semaphore()
    for target in ({"ctx": left}, {"ctx": right}, {"phase": partner}):
        pl.semaphore_signal(barrier, inc=1, device_id=target, device_id_type=MESH)
    pl.semaphore_wait(barrier, 3)

    def columns(chunk):
        return pl.ds(chunk * width, width)

    def remote(source, target, slot, device):
        return pltpu.make_async_remote_copy(
            src_ref=source,
            dst_ref=target,
            send_sem=send_sems.at[slot],
            recv_sem=recv_sems.at[slot],
            device_id=device,
            device_id_type=MESH,
        )

    per = hops + 6
    to_right = {"ctx": right}
    to_partner = {"phase": partner}

    def swap(c):
        return remote(
            other_ref.at[:, :, columns(c)], state.at[phase, :, :, columns(c)], c * per, to_partner
        )

    def hop(c, s):
        source = (
            state.at[1, pl.ds(1, 2), :, columns(c)]
            if s == 0
            else chain.at[s - 1, :, :, columns(c)]
        )
        return remote(source, chain.at[s, :, :, columns(c)], c * per + 6 + s, to_right)

    def send_halo(c):
        rows_ref = state.at[0, :, pl.ds(rows - HALO, HALO), columns(c)]
        return remote(rows_ref, halo.at[:, :, columns(c)], c * per + 1, to_right)

    def send_halo2(c):
        rows_ref = short.at[:, pl.ds(rows - HALO, HALO), columns(c)]
        return remote(rows_ref, halo2.at[:, :, columns(c)], c * per + 2, to_right)

    def send_past(c):
        return remote(tail.at[:, columns(c)], past.at[:, columns(c)], c * per + 3, to_right)

    def send_pair(c):
        return remote(
            state.at[phase, pl.ds(0, 2), :, columns(c)],
            got_ref.at[pl.ds(0, 2), :, columns(c)],
            c * per + 4,
            to_partner,
        )

    def send_value(c):
        return remote(
            state.at[phase, pl.ds(2, 1), :, columns(c)],
            got_ref.at[pl.ds(2, 1), :, columns(c)],
            c * per + 5,
            to_partner,
        )

    def keep(c):
        return pltpu.make_async_copy(
            state.at[partner, :, :, columns(c)], kept_ref.at[:, :, columns(c)], local_sems.at[1 + c]
        )

    for c in range(CHUNKS):
        swap(c).start()

    row = lax.broadcasted_iota(jnp.int32, (rows, keys), 0)
    column = lax.broadcasted_iota(jnp.int32, (rows, keys), 1)
    allowed = (column - rows * hops <= row) & (key_doc_ref[...] == query_doc_ref[...])
    bias_ref[...] = jnp.where(allowed, 0.0, -1e30)

    def over_tiles(chunk, body):
        def one(index, carry):
            body(pl.ds(pl.multiple_of(chunk * width + index * LANES, LANES), LANES))
            return carry

        lax.fori_loop(0, tiles, one, 0)

    def earlier(block):
        return jnp.where(begin, 0.0, block.astype(jnp.float32))

    def short_tile(col):
        weight = feat_ref[:, :, col]

        def wide(stream):
            return jnp.concatenate(
                [earlier(halo[stream, :, col]), state[0, stream, :, col].astype(jnp.float32)], 0
            )

        count = rows + 8
        query = feature(wide(0), weight, 0, rows)
        key = feature(wide(1), weight, 1, count)
        value = feature(wide(2), weight, 2, count)
        product = (key * value).astype(jnp.bfloat16).astype(jnp.float32)
        filt = filt_ref[:, col]
        mixed = filt[0][None] * product[8:]
        for j in range(1, filt_ref.shape[0]):
            mixed += filt[j][None] * product[8 - j : 8 - j + rows]
        new_key = key[8:].astype(jnp.bfloat16)
        new_value = (state[0, 2, :, col].astype(jnp.float32) + query * mixed).astype(jnp.bfloat16)
        short[0, :, col] = query.astype(jnp.bfloat16)
        short[1, :, col] = new_key
        short[2, :, col] = new_value
        weight2 = feat2_ref[:, :, col]
        tail_key = feature(new_key.astype(jnp.float32), weight2, 1, taps)
        tail_value = feature(new_value.astype(jnp.float32), weight2, 2, taps)
        tail[:, col] = (tail_key * tail_value).astype(jnp.bfloat16)

    def medium_tile(col):
        weight = feat2_ref[:, :, col]

        def wide(stream):
            return jnp.concatenate(
                [earlier(halo2[stream, :, col]), short[stream, :, col].astype(jnp.float32)], 0
            )

        query = feature(wide(0), weight, 0, rows)
        key = feature(wide(1), weight, 1, rows)
        value = feature(wide(2), weight, 2, rows)
        state[0, 0, :, col] = query.astype(jnp.bfloat16)
        state[0, 1, :, col] = key.astype(jnp.bfloat16)
        shift_ref[0, :taps] = earlier(past[:, col])
        shift_ref[0, taps:] = (key * value).astype(jnp.bfloat16).astype(jnp.float32)
        length = taps + rows
        for r in range(1, 8):
            shift_ref[r, 8:] = shift_ref[0, 8 - r : length - r]
        position = lax.broadcasted_iota(jnp.int32, (taps, LANES), 0).astype(jnp.float32)
        h_ref[...] = filt2_ref[:, col] * jnp.exp(-rate_ref[:, col] * position)

        def step(m, total):
            weights = h_ref[pl.ds(pl.multiple_of(8 * m, 8), 8), :]
            first = pl.multiple_of(taps - 8 * m, 8)
            for r in range(8):
                total += weights[r : r + 1] * shift_ref[r, pl.ds(first, rows), :]
            return total

        mixed = lax.fori_loop(0, taps // 8, step, jnp.zeros((rows, LANES), jnp.float32))
        total = short[2, :, col].astype(jnp.float32) + query * mixed
        state[0, 2, :, col] = total.astype(jnp.bfloat16)

    def attention_tile(col):
        scale = 1.0 / math.sqrt(HEAD_DIM)
        order = list(range(hops))[::-1]
        key = jnp.concatenate([chain[s, 0, :, col] for s in order] + [state[1, 1, :, col]], 0)
        value = jnp.concatenate([chain[s, 1, :, col] for s in order] + [state[1, 2, :, col]], 0)
        scores = lax.dot_general(
            state[1, 0, :, col], key, (((1,), (1,)), ((), ())), preferred_element_type=jnp.float32
        )
        scores = scores * scale + bias_ref[...]
        exponent = jnp.exp(scores - jnp.max(scores, axis=1, keepdims=True))
        total = jnp.sum(exponent, axis=1, keepdims=True)
        attended = jnp.dot(exponent.astype(jnp.bfloat16), value, preferred_element_type=jnp.float32)
        attended = (attended / total).astype(jnp.bfloat16).astype(jnp.float32)
        summed = state[1, 2, :, col].astype(jnp.float32) + attended
        state[1, 2, :, col] = summed.astype(jnp.bfloat16)

    load_own.wait()
    last = 2 * (CHUNKS - 1) + hops
    for slot in range(last + 2):
        for c in range(CHUNKS):
            age = slot - 2 * c
            if age == 0:
                swap(c).wait_recv()
                hop(c, 0).start()
                send_halo(c).start()
            if 1 <= age <= hops:
                hop(c, age - 1).wait_recv()
                if age < hops:
                    hop(c, age).start()
            if age == 3:
                send_pair(c).start()
            if age == hops + 1:
                send_value(c).start()
                keep(c).start()
        for c in range(CHUNKS):
            age = slot - 2 * c
            if age == 1:
                send_halo(c).wait_recv()
                over_tiles(c, short_tile)
                send_halo2(c).start()
                send_past(c).start()
        for c in range(CHUNKS):
            age = slot - 2 * c
            if age == hops:
                hop(c, 0).wait_send()
                over_tiles(c, attention_tile)
        for c in range(CHUNKS):
            age = slot - 2 * c
            if age == 2:
                send_halo2(c).wait_recv()
                send_past(c).wait_recv()
                send_halo(c).wait_send()
                over_tiles(c, medium_tile)

    for c in range(CHUNKS):
        swap(c).wait_send()
        send_halo2(c).wait_send()
        send_past(c).wait_send()
        for s in range(1, hops):
            hop(c, s).wait_send()
        keep(c).wait()
        send_pair(c).wait()
        send_value(c).wait()


def local(streams, doc_ids, feat_short, filt_short, feat_medium, filt_medium, medium_rates):
    rows = streams.shape[1]
    channels = streams.shape[3]
    half = channels // 2
    taps = filt_medium.shape[0]
    first = lax.axis_index("phase") == 0
    seq_total = rows * lax.axis_size("ctx")
    hops = -(-(seq_total // 2 - 1) // rows)
    keys = (hops + 1) * rows
    start = lax.axis_index("ctx") * rows
    padded_doc = jnp.concatenate([jnp.full((hops * rows,), -1, jnp.int32), doc_ids], 0)
    key_doc = lax.dynamic_slice_in_dim(padded_doc, start, keys, 0)[None]
    query_doc = key_doc[0, hops * rows :][:, None]

    def mine(array):
        return jnp.where(first, array[..., half:], array[..., :half])

    def theirs(array):
        return jnp.where(first, array[..., :half], array[..., half:])

    state = jnp.transpose(streams[0], (1, 0, 2))
    anywhere = pl.BlockSpec(memory_space=pl.ANY)
    inside = pl.BlockSpec(memory_space=pltpu.VMEM)
    shape = jax.ShapeDtypeStruct((3, rows, half), jnp.bfloat16)
    slots = CHUNKS * (hops + 6)
    kept, got = pl.pallas_call(
        functools.partial(tick_kernel, hops),
        in_specs=[anywhere] * 2 + [inside] * 7,
        out_specs=[anywhere] * 2,
        out_shape=[shape, shape],
        scratch_shapes=[
            pltpu.VMEM((2, 3, rows, half), jnp.bfloat16),
            pltpu.VMEM((hops, 2, rows, half), jnp.bfloat16),
            pltpu.VMEM((3, HALO, half), jnp.bfloat16),
            pltpu.VMEM((3, HALO, half), jnp.bfloat16),
            pltpu.VMEM((taps, half), jnp.bfloat16),
            pltpu.VMEM((3, rows, half), jnp.bfloat16),
            pltpu.VMEM((taps, half), jnp.bfloat16),
            pltpu.VMEM((8, taps + rows, LANES), jnp.float32),
            pltpu.VMEM((taps, LANES), jnp.float32),
            pltpu.VMEM((rows, keys), jnp.float32),
            pltpu.SemaphoreType.DMA((1 + CHUNKS,)),
            pltpu.SemaphoreType.DMA((slots,)),
            pltpu.SemaphoreType.DMA((slots,)),
        ],
        compiler_params=pltpu.CompilerParams(
            collective_id=0, has_side_effects=True, vmem_limit_bytes=62 * 1024 * 1024
        ),
    )(
        mine(state),
        theirs(state),
        query_doc,
        key_doc,
        mine(feat_short),
        mine(filt_short),
        mine(feat_medium),
        mine(filt_medium),
        mine(medium_rates)[None],
    )
    low = jnp.where(first, got, kept)
    high = jnp.where(first, kept, got)
    return jnp.transpose(jnp.concatenate([low, high], 2), (1, 0, 2))[None]


def solution(mesh):
    in_specs = (
        P("phase", "ctx", None, "mp"),
        P(),
        P(None, None, "mp"),
        P(None, "mp"),
        P(None, None, "mp"),
        P(None, "mp"),
        P("mp"),
    )
    out_specs = P("phase", "ctx", None, "mp")
    return jax.shard_map(local, mesh=mesh, in_specs=in_specs, out_specs=out_specs, check_vma=False)
```

time: 598 us -> 130 us (0.22)
  the two profiles are of different devices: /device:TPU:10 before, /device:TPU:0 now
where the time goes in v1:
time: 130 us
  Pallas kernels  111 us (85%)
  other arithmetic  17.6 us (14%)
  local copies, waits for them, and re-layouts  1.55 us (1%)
    pallas_call x1, Pallas kernels, local(): pl.pallas_call(functools.partial(tick_kernel, hops), in_specs=[anywhere]...  111 us
    select_n x4, other arithmetic, mine(): return jnp.where(first, array[..., half:], array[..., :half])  7.26 us
    select_n x1, other arithmetic, theirs(): return jnp.where(first, array[..., :half], array[..., half:])  4.88 us
    broadcast_in_dim x1, other arithmetic, local(): return jnp.transpose(jnp.concatenate([low, high], 2), (1, 0, 2))[None]  2.76 us
    select_n x1, other arithmetic, local(): low = jnp.where(first, got, kept)  2.69 us

profile of v1, /device:TPU:0, one launch (start us, length us, event | category | flops | bytes accessed | tf_op | source)
XLA Modules:
  0.0 129.8 jit_solution(16807492536284005436)
XLA Ops:
  0.0 0.8 pad_dynamic-slice_fusion
  0.8 0.0 copy-start
  0.8 1.3 %slice_select_fusion.4 = f32[2048]{0:T(1024)} fusion(f32[4096]{0:T(1024)} %param.13, pred[]{:T(512)S(6)} %eq.3), kind=kLoop, calls=%fused_computation.10 | loop fusion | flops 2048 | bytes 24577 | tf_op jit(solution)/shard_map/jit(_where)/select_n | solution.py:295
  2.1 1.5 %slice_select_fusion.3.filt_ref = f32[7,2048]{1,0:T(8,128)} fusion(f32[7,4096]{1,0:T(8,128)} %param.10, pred[]{:T(512)S(6)} %eq.3), kind=kLoop, calls=%fused_computation.8 | loop fusion | flops 14336 | bytes 172033 | tf_op jit(solution)/shard_map/jit(_where)/select_n | solution.py:295
  3.6 0.8 copy.8.query_doc_ref
  4.4 1.8 %slice_select_fusion.1 = (f32[3,3,2048]{2,1,0:T(4,128)}, f32[3,3,2048]{2,1,0:T(4,128)}) fusion(f32[3,3,4096]{2,1,0:T(4,128)} %param.11, pred[]{:T(512)S(6)} %eq.3, f32[3,3,4096]{2,1,0:T(4,128)} %param.9), kind=kLoop, calls=%fused_computation.6 | loop fusion | flops 36864 | bytes 442369 | tf_op jit(solution)/shard_map/jit(_where)/select_n | solution.py:295
  6.2 2.6 %slice_select_fusion.filt2_ref = f32[128,2048]{1,0:T(8,128)} fusion(f32[128,4096]{1,0:T(8,128)} %param.12, pred[]{:T(512)S(6)} %eq.3), kind=kLoop, calls=%fused_computation.5 | loop fusion | flops 262144 | bytes 3145729 | tf_op jit(solution)/shard_map/jit(_where)/select_n | solution.py:295
  8.8 4.9 %broadcast_select_fusion.2 = (bf16[3,192,2048]{2,1,0:T(8,128)(2,1)}, bf16[3,192,2048]{2,1,0:T(8,128)(2,1)}) fusion(pred[]{:T(512)S(6)} %eq.3, bf16[3,192,4096]{2,1,0:T(8,128)(2,1)} %bitcast.11), kind=kLoop, calls=%fused_computation.3 | loop fusion | flops 2359296 | bytes 9437185 | tf_op jit(solution)/shard_map/jit(_where)/select_n | solution.py:298
  13.7 0.0 copy-done
  13.7 110.7 %shard_map.73 = (bf16[3,192,2048]{2,1,0:T(8,128)(2,1)}, bf16[3,192,2048]{2,1,0:T(8,128)(2,1)}) custom-call(bf16[3,192,2048]{2,1,0:T(8,128)(2,1)} %get-tuple-element.12.own_ref, bf16[3,192,2048]{2,1,0:T(8,128)(2,1)} %get-tuple-element.11.other_ref, s32[192,1]{1,0:T(8,128)} %copy.8.query_doc_ref, s32[1,960]{1,0:T(1,128)} %bitcast.14, ...), custom_call_target="tpu_custom_call" | custom-call | tf_op jit(solution)/shard_map/pallas_call | solution.py:305
  124.4 2.7 %broadcast_select_fusion.1 = (bf16[3,192,2048]{2,1,0:T(8,128)(2,1)S(1)}, bf16[3,192,2048]{2,1,0:T(8,128)(2,1)S(1)}) fusion(bf16[3,192,2048]{2,1,0:T(8,128)(2,1)} %get-tuple-element.7, bf16[3,192,2048]{2,1,0:T(8,128)(2,1)} %get-tuple-element.8, pred[]{:T(512)S(6)} %eq.3), kind=kLoop, calls=%fused_computation.2 | loop fusion | flops 2359296 | bytes 9437185 | tf_op jit(solution)/shard_map/jit(_where)/select_n | solution.py:339
  127.1 2.8 %maximum_bitcast_fusion = bf16[1,192,3,4096]{3,1,2,0:T(8,128)(2,1)} fusion(bf16[3,192,2048]{2,1,0:T(8,128)(2,1)S(1)} %get-tuple-element.10, bf16[3,192,2048]{2,1,0:T(8,128)(2,1)S(1)} %get-tuple-element.9), kind=kLoop, calls=%fused_computation | loop fusion | flops 9437184 | bytes 9437184 | tf_op jit(solution)/shard_map/broadcast_in_dim | solution.py:341
  (1 shorter events, 0.0 us)
Async XLA Ops:
  0.8 12.9 %copy-start = (s32[960]{0:T(1024)}, s32[960]{0:T(1024)S(1)}, u32[]{:S(2)}) copy-start(s32[960]{0:T(1024)S(1)} %pad_dynamic-slice_fusion) | copy-start | bytes 11524

commit v2 on v1

--- a/solution.py
+++ b/solution.py
@@ -26,17 +26,19 @@
 
 def tick_kernel(
     hops,
-    own_ref,
-    other_ref,
-    query_doc_ref,
+    whole_ref,
     key_doc_ref,
+    feat_all,
+    filt_all,
+    feat2_all,
+    filt2_all,
+    rate_all,
+    out_ref,
     feat_ref,
     filt_ref,
     feat2_ref,
     filt2_ref,
     rate_ref,
-    kept_ref,
-    got_ref,
     state,
     chain,
     halo,
@@ -65,8 +67,26 @@
     partner = 1 - phase
     begin = place == 0
 
-    load_own = pltpu.make_async_copy(own_ref, state.at[phase], local_sems.at[0])
-    load_own.start()
+    mine = partner * half
+    theirs = phase * half
+
+    def piece(offset, size):
+        return pl.ds(pl.multiple_of(offset, LANES), size)
+
+    loads = [
+        pltpu.make_async_copy(
+            whole_ref.at[:, :, piece(mine, half)], state.at[phase], local_sems.at[CHUNKS]
+        )
+    ]
+    pairs = (
+        (feat_all.at[:, :, piece(mine, half)], feat_ref),
+        (filt_all.at[:, piece(mine, half)], filt_ref),
+        (feat2_all.at[:, :, piece(mine, half)], feat2_ref),
+        (filt2_all.at[:, piece(mine, half)], filt2_ref),
+        (rate_all.at[:, piece(mine, half)], rate_ref),
+    )
+    for index, (source, target) in enumerate(pairs):
+        loads.append(pltpu.make_async_copy(source, target, local_sems.at[CHUNKS + 1 + index]))
 
     barrier = pltpu.get_barrier_semaphore()
     for target in ({"ctx": left}, {"ctx": right}, {"phase": partner}):
@@ -92,7 +112,7 @@
 
     def swap(c):
         return remote(
-            other_ref.at[:, :, columns(c)], state.at[phase, :, :, columns(c)], c * per, to_partner
+            whole_ref.at[:, :, piece(theirs + c * width, width)], state.at[phase, :, :, columns(c)], c * per, to_partner
         )
 
     def hop(c, s):
@@ -117,7 +137,7 @@
     def send_pair(c):
         return remote(
             state.at[phase, pl.ds(0, 2), :, columns(c)],
-            got_ref.at[pl.ds(0, 2), :, columns(c)],
+            out_ref.at[pl.ds(0, 2), :, piece(mine + c * width, width)],
             c * per + 4,
             to_partner,
         )
@@ -125,22 +145,32 @@
     def send_value(c):
         return remote(
             state.at[phase, pl.ds(2, 1), :, columns(c)],
-            got_ref.at[pl.ds(2, 1), :, columns(c)],
+            out_ref.at[pl.ds(2, 1), :, piece(mine + c * width, width)],
             c * per + 5,
             to_partner,
         )
 
     def keep(c):
         return pltpu.make_async_copy(
-            state.at[partner, :, :, columns(c)], kept_ref.at[:, :, columns(c)], local_sems.at[1 + c]
+            state.at[partner, :, :, columns(c)],
+            out_ref.at[:, :, piece(mine + c * width, width)],
+            local_sems.at[c],
         )
 
     for c in range(CHUNKS):
         swap(c).start()
+    for load in loads:
+        load.start()
 
     row = lax.broadcasted_iota(jnp.int32, (rows, keys), 0)
     column = lax.broadcasted_iota(jnp.int32, (rows, keys), 1)
-    allowed = (column - rows * hops <= row) & (key_doc_ref[...] == query_doc_ref[...])
+    key_doc = key_doc_ref[...].astype(jnp.float32)
+    across = lax.broadcasted_iota(jnp.int32, (rows, rows), 1)
+    down = lax.broadcasted_iota(jnp.int32, (rows, rows), 0)
+    query_doc = jnp.sum(
+        jnp.where(across == down, key_doc[:, rows * hops :], 0.0), axis=1, keepdims=True
+    )
+    allowed = (column - rows * hops <= row) & (key_doc == query_doc)
     bias_ref[...] = jnp.where(allowed, 0.0, -1e30)
 
     def over_tiles(chunk, body):
@@ -228,7 +258,8 @@
         summed = state[1, 2, :, col].astype(jnp.float32) + attended
         state[1, 2, :, col] = summed.astype(jnp.bfloat16)
 
-    load_own.wait()
+    for load in loads:
+        load.wait()
     last = 2 * (CHUNKS - 1) + hops
     for slot in range(last + 2):
         for c in range(CHUNKS):
@@ -282,32 +313,27 @@
     channels = streams.shape[3]
     half = channels // 2
     taps = filt_medium.shape[0]
-    first = lax.axis_index("phase") == 0
     seq_total = rows * lax.axis_size("ctx")
     hops = -(-(seq_total // 2 - 1) // rows)
     keys = (hops + 1) * rows
     start = lax.axis_index("ctx") * rows
     padded_doc = jnp.concatenate([jnp.full((hops * rows,), -1, jnp.int32), doc_ids], 0)
     key_doc = lax.dynamic_slice_in_dim(padded_doc, start, keys, 0)[None]
-    query_doc = key_doc[0, hops * rows :][:, None]
-
-    def mine(array):
-        return jnp.where(first, array[..., half:], array[..., :half])
-
-    def theirs(array):
-        return jnp.where(first, array[..., :half], array[..., half:])
-
     state = jnp.transpose(streams[0], (1, 0, 2))
     anywhere = pl.BlockSpec(memory_space=pl.ANY)
     inside = pl.BlockSpec(memory_space=pltpu.VMEM)
-    shape = jax.ShapeDtypeStruct((3, rows, half), jnp.bfloat16)
     slots = CHUNKS * (hops + 6)
-    kept, got = pl.pallas_call(
+    out = pl.pallas_call(
         functools.partial(tick_kernel, hops),
-        in_specs=[anywhere] * 2 + [inside] * 7,
-        out_specs=[anywhere] * 2,
-        out_shape=[shape, shape],
+        in_specs=[anywhere, inside] + [anywhere] * 5,
+        out_specs=anywhere,
+        out_shape=jax.ShapeDtypeStruct((3, rows, channels), jnp.bfloat16),
         scratch_shapes=[
+            pltpu.VMEM((3, 3, half), jnp.float32),
+            pltpu.VMEM((filt_short.shape[0], half), jnp.float32),
+            pltpu.VMEM((3, 3, half), jnp.float32),
+            pltpu.VMEM((taps, half), jnp.float32),
+            pltpu.VMEM((1, half), jnp.float32),
             pltpu.VMEM((2, 3, rows, half), jnp.bfloat16),
             pltpu.VMEM((hops, 2, rows, half), jnp.bfloat16),
             pltpu.VMEM((3, HALO, half), jnp.bfloat16),
@@ -318,7 +344,7 @@
             pltpu.VMEM((8, taps + rows, LANES), jnp.float32),
             pltpu.VMEM((taps, LANES), jnp.float32),
             pltpu.VMEM((rows, keys), jnp.float32),
-            pltpu.SemaphoreType.DMA((1 + CHUNKS,)),
+            pltpu.SemaphoreType.DMA((CHUNKS + 6,)),
             pltpu.SemaphoreType.DMA((slots,)),
             pltpu.SemaphoreType.DMA((slots,)),
         ],
@@ -326,19 +352,15 @@
             collective_id=0, has_side_effects=True, vmem_limit_bytes=62 * 1024 * 1024
         ),
     )(
-        mine(state),
-        theirs(state),
-        query_doc,
+        state,
         key_doc,
-        mine(feat_short),
-        mine(filt_short),
-        mine(feat_medium),
-        mine(filt_medium),
-        mine(medium_rates)[None],
-    )
-    low = jnp.where(first, got, kept)
-    high = jnp.where(first, kept, got)
-    return jnp.transpose(jnp.concatenate([low, high], 2), (1, 0, 2))[None]
+        feat_short,
+        filt_short,
+        feat_medium,
+        filt_medium,
+        medium_rates[None],
+    )
+    return jnp.transpose(out, (1, 0, 2))[None]
 
 
 def solution(mesh):

time: 130 us -> 117 us (0.900)
  other arithmetic: 17.6 us -> 0 us
  local copies, waits for them, and re-layouts: 1.55 us -> 6.46 us
    select_n x6 -> x0, other arithmetic: 14.8 us -> none  [the longest x4 7.26 us: mine(): return jnp.where(first, array[..., half:], array[..., :half])]
    unnamed x2 -> x1, local copies, waits for them, and re-layouts: 0.01 us -> 5.09 us
    broadcast_in_dim x1 -> x0, other arithmetic: 2.76 us -> none  [local(): return jnp.transpose(jnp.concatenate([low, high], 2), (1, 0, 2))[None]]
where the time goes in v2:
time: 117 us
  Pallas kernels  110 us (94%)
  local copies, waits for them, and re-layouts  6.46 us (6%)
    pallas_call x1, Pallas kernels, local(): pl.pallas_call(functools.partial(tick_kernel, hops), in_specs=[anywhere,...  110 us
    unnamed x1, local copies, waits for them, and re-layouts  5.09 us

profile of v2, /device:TPU:0, one launch (start us, length us, event | category | flops | bytes accessed | tf_op | source)
XLA Modules:
  0.0 116.5 jit_solution(7906860456392687714)
XLA Ops:
  0.0 1.4 %pad_dynamic-slice_fusion = s32[960]{0:T(1024)} fusion(s32[]{:T(128)S(6)} %select_n.3, s32[1536]{0:T(1024)} %param.8), kind=kLoop, calls=%fused_computation | loop fusion | bytes 9988 | tf_op jit(solution)/shard_map/dynamic_slice | solution.py:321
  1.4 110.1 %shard_map.73 = bf16[3,192,4096]{2,1,0:T(8,128)(2,1)} custom-call(bf16[3,192,4096]{2,1,0:T(8,128)(2,1)} %bitcast.9, s32[1,960]{1,0:T(1,128)} %bitcast.11, f32[3,3,4096]{2,1,0:T(4,128)} %feat_all.1, f32[7,4096]{1,0:T(8,128)} %filt_all.1, f32[3,3,4096]{2,1,0:T(4,128)} %feat2_all.1, f32[128,4096]{1,0:T(8,128)} %filt2_all.1, f32[1,4096]{1,0:T(1,128)} %bitcast.10), custom_call_target="tpu_custom_call" | custom-call | tf_op jit(solution)/shard_map/pallas_call | solution.py:326
  111.5 5.1 %copy.9 = bf16[1,192,3,4096]{3,1,2,0:T(8,128)(2,1)} copy(bf16[1,192,3,4096]{3,1,2,0:T(8,128)(2,1)} %bitcast.8) | data formatting | bytes 9437184

commit v3 on v2

--- a/solution.py
+++ b/solution.py
@@ -11,6 +11,7 @@
 HEAD_DIM = 128
 CHUNKS = 4
 HALO = 16
+PIECES = 4
 LANES = 128
 MESH = pl.DeviceIdType.MESH
 
@@ -62,10 +63,9 @@
     phase = lax.axis_index("phase")
     place = lax.axis_index("ctx")
     peers = lax.axis_size("ctx")
-    right = lax.rem(place + 1, peers)
-    left = lax.rem(place + peers - 1, peers)
+    right, left = place + 1, place - 1
     partner = 1 - phase
-    begin = place == 0
+    has_left, has_right = place > 0, place < peers - 1
 
     mine = partner * half
     theirs = phase * half
@@ -89,9 +89,18 @@
         loads.append(pltpu.make_async_copy(source, target, local_sems.at[CHUNKS + 1 + index]))
 
     barrier = pltpu.get_barrier_semaphore()
-    for target in ({"ctx": left}, {"ctx": right}, {"phase": partner}):
-        pl.semaphore_signal(barrier, inc=1, device_id=target, device_id_type=MESH)
-    pl.semaphore_wait(barrier, 3)
+    pl.semaphore_signal(barrier, inc=1, device_id={"phase": partner}, device_id_type=MESH)
+
+    @pl.when(has_left)
+    def _():
+        pl.semaphore_signal(barrier, inc=1, device_id={"ctx": left}, device_id_type=MESH)
+
+    @pl.when(has_right)
+    def _():
+        pl.semaphore_signal(barrier, inc=1, device_id={"ctx": right}, device_id_type=MESH)
+
+    inner = (place + peers - 1) // peers + (peers - 1 - place + peers - 1) // peers
+    pl.semaphore_wait(barrier, 1 + inner)
 
     def columns(chunk):
         return pl.ds(chunk * width, width)
@@ -161,6 +170,39 @@
         swap(c).start()
     for load in loads:
         load.start()
+
+    @pl.when(place == 0)
+    def _():
+        halo[...] = jnp.zeros_like(halo)
+        halo2[...] = jnp.zeros_like(halo2)
+        past[...] = jnp.zeros_like(past)
+
+    for s in range(hops):
+
+        @pl.when(place <= s)
+        def _():
+            chain[s] = jnp.zeros(chain.shape[1:], chain.dtype)
+
+    def start(condition, *copies):
+        @pl.when(condition)
+        def _():
+            for copy in copies:
+                copy.start()
+
+    def sent(condition, *copies):
+        @pl.when(condition)
+        def _():
+            for copy in copies:
+                copy.wait_send()
+
+    def arrived(condition, *copies):
+        @pl.when(condition)
+        def _():
+            for copy in copies:
+                copy.wait_recv()
+
+    def sends_hop(s):
+        return has_right & (place >= s)
 
     row = lax.broadcasted_iota(jnp.int32, (rows, keys), 0)
     column = lax.broadcasted_iota(jnp.int32, (rows, keys), 1)
@@ -181,7 +223,7 @@
         lax.fori_loop(0, tiles, one, 0)
 
     def earlier(block):
-        return jnp.where(begin, 0.0, block.astype(jnp.float32))
+        return block.astype(jnp.float32)
 
     def short_tile(col):
         weight = feat_ref[:, :, col]
@@ -266,12 +308,11 @@
             age = slot - 2 * c
             if age == 0:
                 swap(c).wait_recv()
-                hop(c, 0).start()
-                send_halo(c).start()
+                start(has_right, hop(c, 0), send_halo(c))
             if 1 <= age <= hops:
-                hop(c, age - 1).wait_recv()
+                arrived(place >= age, hop(c, age - 1))
                 if age < hops:
-                    hop(c, age).start()
+                    start(sends_hop(age), hop(c, age))
             if age == 3:
                 send_pair(c).start()
             if age == hops + 1:
@@ -280,32 +321,66 @@
         for c in range(CHUNKS):
             age = slot - 2 * c
             if age == 1:
-                send_halo(c).wait_recv()
+                arrived(has_left, send_halo(c))
                 over_tiles(c, short_tile)
-                send_halo2(c).start()
-                send_past(c).start()
+                start(has_right, send_halo2(c), send_past(c))
         for c in range(CHUNKS):
             age = slot - 2 * c
             if age == hops:
-                hop(c, 0).wait_send()
+                sent(has_right, hop(c, 0))
                 over_tiles(c, attention_tile)
         for c in range(CHUNKS):
             age = slot - 2 * c
             if age == 2:
-                send_halo2(c).wait_recv()
-                send_past(c).wait_recv()
-                send_halo(c).wait_send()
+                arrived(has_left, send_halo2(c), send_past(c))
+                sent(has_right, send_halo(c))
                 over_tiles(c, medium_tile)
 
     for c in range(CHUNKS):
         swap(c).wait_send()
-        send_halo2(c).wait_send()
-        send_past(c).wait_send()
+        sent(has_right, send_halo2(c), send_past(c))
         for s in range(1, hops):
-            hop(c, s).wait_send()
+            sent(sends_hop(s), hop(c, s))
         keep(c).wait()
         send_pair(c).wait()
         send_value(c).wait()
+
+
+def copy_kernel(source, target, held, in_sems, out_sems):
+    streams, rows, _ = source.shape
+    size = rows // PIECES
+    parts = [(i, pl.ds(j * size, size)) for i in range(streams) for j in range(PIECES)]
+    ins = [
+        pltpu.make_async_copy(source.at[part], held.at[part], in_sems.at[n])
+        for n, part in enumerate(parts)
+    ]
+    outs = [
+        pltpu.make_async_copy(held.at[part], target.at[part], out_sems.at[n])
+        for n, part in enumerate(parts)
+    ]
+    for copy in ins:
+        copy.start()
+    for first, second in zip(ins, outs):
+        first.wait()
+        second.start()
+    for copy in outs:
+        copy.wait()
+
+
+def copied(array):
+    anywhere = pl.BlockSpec(memory_space=pl.ANY)
+    count = array.shape[0] * PIECES
+    return pl.pallas_call(
+        copy_kernel,
+        in_specs=[anywhere],
+        out_specs=anywhere,
+        out_shape=jax.ShapeDtypeStruct(array.shape, array.dtype),
+        scratch_shapes=[
+            pltpu.VMEM(array.shape, array.dtype),
+            pltpu.SemaphoreType.DMA((count,)),
+            pltpu.SemaphoreType.DMA((count,)),
+        ],
+    )(array)
 
 
 def local(streams, doc_ids, feat_short, filt_short, feat_medium, filt_medium, medium_rates):
@@ -360,7 +435,7 @@
         filt_medium,
         medium_rates[None],
     )
-    return jnp.transpose(out, (1, 0, 2))[None]
+    return jnp.transpose(copied(out), (1, 0, 2))[None]
 
 
 def solution(mesh):

time: 117 us -> 113 us (0.966)
  local copies, waits for them, and re-layouts: 6.46 us -> 1.36 us
    unnamed x1 -> x0, local copies, waits for them, and re-layouts: 5.09 us -> none
    pallas_call x0 -> x1, Pallas kernels: none -> 4.27 us  [copied(): pl.pallas_call(copy_kernel, in_specs=[anywhere], out_specs=anywhere, out_...]
    pallas_call x1, Pallas kernels: 110 us -> 106 us  [local(): pl.pallas_call(functools.partial(tick_kernel, hops), in_specs=[anywhere,...]
where the time goes in v3:
time: 113 us; the launch traced here: 112 us
  Pallas kernels  111 us (98%)
  local copies, waits for them, and re-layouts  1.36 us (1%)
    pallas_call x1, Pallas kernels, local(): pl.pallas_call(functools.partial(tick_kernel, hops), in_specs=[anywhere,...  106 us
    pallas_call x1, Pallas kernels, copied(): pl.pallas_call(copy_kernel, in_specs=[anywhere], out_specs=anywhere, out_...  4.27 us

profile of v3, /device:TPU:0, one launch (start us, length us, event | category | flops | bytes accessed | tf_op | source)
XLA Modules:
  0.0 112.1 jit_solution(5088771207657684291)
XLA Ops:
  0.0 1.4 %pad_dynamic-slice_fusion = s32[960]{0:T(1024)} fusion(s32[]{:T(128)S(6)} %select_n.3, s32[1536]{0:T(1024)} %param.8), kind=kLoop, calls=%fused_computation | loop fusion | bytes 9988 | tf_op jit(solution)/shard_map/dynamic_slice | solution.py:396
  1.4 106.4 %shard_map.73.source = bf16[3,192,4096]{2,1,0:T(8,128)(2,1)} custom-call(bf16[3,192,4096]{2,1,0:T(8,128)(2,1)} %bitcast.8, s32[1,960]{1,0:T(1,128)} %bitcast.10, f32[3,3,4096]{2,1,0:T(4,128)} %feat_all.1, f32[7,4096]{1,0:T(8,128)} %filt_all.1, f32[3,3,4096]{2,1,0:T(4,128)} %feat2_all.1, f32[128,4096]{1,0:T(8,128)} %filt2_all.1, f32[1,4096]{1,0:T(1,128)} %bitcast.9), custom_call_target="tpu_custom_call" | custom-call | tf_op jit(solution)/shard_map/pallas_call | solution.py:401
  107.8 4.3 %shard_map.74 = bf16[3,192,4096]{2,1,0:T(8,128)(2,1)} custom-call(bf16[3,192,4096]{2,1,0:T(8,128)(2,1)} %shard_map.73.source), custom_call_target="tpu_custom_call" | custom-call | tf_op jit(solution)/shard_map/pallas_call | solution.py:373

commit v4 on v3

--- a/solution.py
+++ b/solution.py
@@ -9,7 +9,7 @@
 from jax.sharding import PartitionSpec as P
 
 HEAD_DIM = 128
-CHUNKS = 4
+CHUNKS = 8
 HALO = 16
 PIECES = 4
 LANES = 128

time: 113 us -> 113 us (level)
  no operation moved by 1% of the time
where the time goes in v4:
time: 113 us
  Pallas kernels  111 us (98%)
  local copies, waits for them, and re-layouts  1.36 us (1%)
    pallas_call x1, Pallas kernels, local(): pl.pallas_call(functools.partial(tick_kernel, hops), in_specs=[anywhere,...  107 us
    pallas_call x1, Pallas kernels, copied(): pl.pallas_call(copy_kernel, in_specs=[anywhere], out_specs=anywhere, out_...  4.27 us

profile of v4, /device:TPU:0, one launch (start us, length us, event | category | flops | bytes accessed | tf_op | source)
XLA Modules:
  0.0 112.8 jit_solution(2302930194623558138)
XLA Ops:
  0.0 1.4 %pad_dynamic-slice_fusion = s32[960]{0:T(1024)} fusion(s32[]{:T(128)S(6)} %select_n.3, s32[1536]{0:T(1024)} %param.8), kind=kLoop, calls=%fused_computation | loop fusion | bytes 9988 | tf_op jit(solution)/shard_map/dynamic_slice | solution.py:396
  1.4 107.2 %shard_map.73.source = bf16[3,192,4096]{2,1,0:T(8,128)(2,1)} custom-call(bf16[3,192,4096]{2,1,0:T(8,128)(2,1)} %bitcast.8, s32[1,960]{1,0:T(1,128)} %bitcast.10, f32[3,3,4096]{2,1,0:T(4,128)} %feat_all.1, f32[7,4096]{1,0:T(8,128)} %filt_all.1, f32[3,3,4096]{2,1,0:T(4,128)} %feat2_all.1, f32[128,4096]{1,0:T(8,128)} %filt2_all.1, f32[1,4096]{1,0:T(1,128)} %bitcast.9), custom_call_target="tpu_custom_call" | custom-call | tf_op jit(solution)/shard_map/pallas_call | solution.py:401
  108.6 4.3 %shard_map.74 = bf16[3,192,4096]{2,1,0:T(8,128)(2,1)} custom-call(bf16[3,192,4096]{2,1,0:T(8,128)(2,1)} %shard_map.73.source), custom_call_target="tpu_custom_call" | custom-call | tf_op jit(solution)/shard_map/pallas_call | solution.py:373

commit v5 on v3

--- a/solution.py
+++ b/solution.py
@@ -28,7 +28,7 @@
 def tick_kernel(
     hops,
     whole_ref,
-    key_doc_ref,
+    doc_ref,
     feat_all,
     filt_all,
     feat2_all,
@@ -204,16 +204,23 @@
     def sends_hop(s):
         return has_right & (place >= s)
 
-    row = lax.broadcasted_iota(jnp.int32, (rows, keys), 0)
-    column = lax.broadcasted_iota(jnp.int32, (rows, keys), 1)
-    key_doc = key_doc_ref[...].astype(jnp.float32)
-    across = lax.broadcasted_iota(jnp.int32, (rows, rows), 1)
-    down = lax.broadcasted_iota(jnp.int32, (rows, rows), 0)
-    query_doc = jnp.sum(
-        jnp.where(across == down, key_doc[:, rows * hops :], 0.0), axis=1, keepdims=True
-    )
-    allowed = (column - rows * hops <= row) & (key_doc == query_doc)
-    bias_ref[...] = jnp.where(allowed, 0.0, -1e30)
+    column = lax.broadcasted_iota(jnp.int32, (rows, rows), 1)
+    row = lax.broadcasted_iota(jnp.int32, (rows, rows), 0)
+    docs = doc_ref[...].astype(jnp.float32)
+
+    def block_docs(block):
+        found = jnp.full((1, rows), -1.0, jnp.float32)
+        for b in range(peers):
+            found = jnp.where(block == b, docs[:, b * rows : (b + 1) * rows], found)
+        return found
+
+    own_docs = block_docs(place)
+    query_doc = jnp.sum(jnp.where(column == row, own_docs, 0.0), axis=1, keepdims=True)
+    for i in range(hops + 1):
+        allowed = block_docs(place - hops + i) == query_doc
+        if i == hops:
+            allowed = allowed & (column <= row)
+        bias_ref[:, i * rows : (i + 1) * rows] = jnp.where(allowed, 0.0, -1e30)
 
     def over_tiles(chunk, body):
         def one(index, carry):
@@ -391,9 +398,6 @@
     seq_total = rows * lax.axis_size("ctx")
     hops = -(-(seq_total // 2 - 1) // rows)
     keys = (hops + 1) * rows
-    start = lax.axis_index("ctx") * rows
-    padded_doc = jnp.concatenate([jnp.full((hops * rows,), -1, jnp.int32), doc_ids], 0)
-    key_doc = lax.dynamic_slice_in_dim(padded_doc, start, keys, 0)[None]
     state = jnp.transpose(streams[0], (1, 0, 2))
     anywhere = pl.BlockSpec(memory_space=pl.ANY)
     inside = pl.BlockSpec(memory_space=pltpu.VMEM)
@@ -428,7 +432,7 @@
         ),
     )(
         state,
-        key_doc,
+        doc_ids[None],
         feat_short,
         filt_short,
         feat_medium,

time: 113 us -> 113 us (level)
    dynamic_slice x1 -> x0, local copies, waits for them, and re-layouts: 1.36 us -> none  [local(): key_doc = lax.dynamic_slice_in_dim(padded_doc, start, keys, 0)[None]]
    broadcast_in_dim x0 -> x1, local copies, waits for them, and re-layouts: none -> 1.29 us  [local(): doc_ids[None]]
where the time goes in v5:
time: 113 us; the launch traced here: 112 us
  Pallas kernels  111 us (98%)
  local copies, waits for them, and re-layouts  1.29 us (1%)
    pallas_call x1, Pallas kernels, local(): pl.pallas_call(functools.partial(tick_kernel, hops), in_specs=[anywhere,...  106 us
    pallas_call x1, Pallas kernels, copied(): pl.pallas_call(copy_kernel, in_specs=[anywhere], out_specs=anywhere, out_...  4.27 us

profile of v5, /device:TPU:0, one launch (start us, length us, event | category | flops | bytes accessed | tf_op | source)
XLA Modules:
  0.0 112.0 jit_solution(5955731785972858764)
XLA Ops:
  0.0 1.3 %broadcast_in_dim.9.doc_ref = s32[1,1536]{1,0:T(1,128)} reshape(s32[1536]{0:T(1024)} %param.8) | data formatting | bytes 12288 | tf_op jit(solution)/shard_map/broadcast_in_dim | solution.py:435
  1.3 106.4 %shard_map.73.source = bf16[3,192,4096]{2,1,0:T(8,128)(2,1)} custom-call(bf16[3,192,4096]{2,1,0:T(8,128)(2,1)} %bitcast.7, s32[1,1536]{1,0:T(1,128)} %broadcast_in_dim.9.doc_ref, f32[3,3,4096]{2,1,0:T(4,128)} %feat_all.1, f32[7,4096]{1,0:T(8,128)} %filt_all.1, f32[3,3,4096]{2,1,0:T(4,128)} %feat2_all.1, f32[128,4096]{1,0:T(8,128)} %filt2_all.1, ...), custom_call_target="tpu_custom_call" | custom-call | tf_op jit(solution)/shard_map/pallas_call | solution.py:405
  107.7 4.3 %shard_map.74 = bf16[3,192,4096]{2,1,0:T(8,128)(2,1)} custom-call(bf16[3,192,4096]{2,1,0:T(8,128)(2,1)} %shard_map.73.source), custom_call_target="tpu_custom_call" | custom-call | tf_op jit(solution)/shard_map/pallas_call | solution.py:380
